TPU v7x, 512 devices: a whole 4x4x16 slice. The times are simulated.
512 devices in a mesh: dp: 32 (over x_hi, z), spatial: 16 (over x_lo, y, core).
Axes of the slice: x: 4 (x_hi: 2, x_lo: 2; x = x_hi * 2 + x_lo), y: 4, z: 16, core: 2. Of those that a mesh axis runs over, the one named last changes fastest.
Arguments:
- latents: bfloat16 [64, 32, 32, 640], P('dp', 'spatial'), may hold values from -16 to 16
- plan: bfloat16 [64, 256, 640], P('dp', 'spatial'), may hold values from -45 to 45
- conv_weight: bfloat16 [9, 640, 640], P(None, 'dp'), may hold values from -0.078125 to 0.078125
- gn_gain: float32 [640], replicated, may hold values from 0.5 to 2
- attn_weights: bfloat16 [4, 640, 640], P(None, 'dp'), may hold values from -0.25 to 0.25
- cotangent: bfloat16 [64, 32, 32, 640], P('dp', 'spatial'), may hold values from -6 to 6
Outputs:
- block_out: bfloat16 [64, 32, 32, 640], P('dp', 'spatial')
- weight_grads: float32 [640, 2, 640], P('dp')
All inputs are finite; a program needn't handle non-finite values.
Results may differ from a plain program's by a relative error of at most 0.03.
The roundings to bfloat16 on the way count: a program that leaves them out, or rounds other values in their place, can miss the bound.
Values may be sent and summed in bfloat16 or wider, within the bound.
A program may use at most 64 MiB of HBM per device.

v0:
```python
import math
import jax
import jax.numpy as jnp
from jax import lax
from jax.sharding import PartitionSpec as P

GROUPS = 32
HEAD = 64
eps_norm = 1e-05


def with_halo(cells, sides, width):
    for axis, dim in sides:
        count = lax.axis_size(axis)
        ends = count - 1
        head = lax.slice_in_dim(cells, 0, width, axis=dim)
        tail = lax.slice_in_dim(cells, cells.shape[dim] - width, cells.shape[dim], axis=dim)
        cells = jnp.concatenate(
            [
                lax.ppermute(tail, axis, [(i, (i + 1) % count) for i in range(ends)]),
                cells,
                lax.ppermute(head, axis, [((i + 1) % count, i) for i in range(ends)]),
            ],
            axis=dim,
        )
    return cells


def body(latents, plan, conv_weight, gn_gain, attn_weights, cotangent):
    images, band_rows, columns, channels = latents.shape
    heads = channels // HEAD
    per_group = channels // GROUPS
    tokens_here = images * band_rows * columns
    scale = 1.0 / math.sqrt(HEAD)
    flat_input = latents.astype(jnp.float32).reshape(images, band_rows * columns, GROUPS, per_group)
    first_sums = jnp.sum(flat_input, axis=(1, 3))
    second_sums = jnp.sum(flat_input * flat_input, axis=(1, 3))
    first_sums, second_sums = lax.psum((first_sums, second_sums), "spatial")
    counted = float(band_rows * lax.axis_size("spatial") * columns * per_group)
    means = first_sums / counted
    variance = second_sums / counted - means * means
    inverse = lax.rsqrt(variance + eps_norm)
    normed = (flat_input - means[:, None, :, None]) * inverse[:, None, :, None]
    normed = normed.reshape(images, band_rows, columns, channels) * gn_gain
    hidden = jax.nn.silu(normed).astype(jnp.bfloat16)
    padded = with_halo(hidden, (("spatial", 1),), 1)
    padded = jnp.pad(padded, ((0, 0), (0, 0), (1, 1), (0, 0)))
    tapped = jnp.stack(
        [
            padded[:, offset_y : offset_y + band_rows, offset_x : offset_x + columns].reshape(
                tokens_here, channels
            )
            for offset_y in range(3)
            for offset_x in range(3)
        ],
        1,
    )
    conv_sum = jnp.einsum(
        "ntc,tcd->nd",
        tapped,
        lax.all_gather(conv_weight, "dp", axis=1, tiled=True),
        preferred_element_type=jnp.float32,
    )
    mixed = (latents.reshape(tokens_here, channels).astype(jnp.float32) + conv_sum).astype(
        jnp.bfloat16
    )
    weights = lax.all_gather(attn_weights, "dp", axis=1, tiled=True)
    weight_q = weights[0]
    weight_k = weights[1]
    weight_v = weights[2]
    weight_o = weights[3]
    queries = jnp.dot(mixed, weight_q, preferred_element_type=jnp.float32).astype(jnp.bfloat16)
    plan_all = lax.all_gather(plan, "spatial", axis=1, tiled=True)
    plan_flat = plan_all.reshape(-1, channels)
    keys_all = jnp.dot(plan_flat, weight_k, preferred_element_type=jnp.float32).astype(jnp.bfloat16)
    values_all = jnp.dot(plan_flat, weight_v, preferred_element_type=jnp.float32).astype(
        jnp.bfloat16
    )
    keys_all = keys_all.reshape(images, -1, channels)
    values_all = values_all.reshape(images, -1, channels)
    plan_tokens = keys_all.shape[1]
    query_heads = queries.reshape(images, band_rows * columns, heads, HEAD)
    key_heads = keys_all.reshape(images, plan_tokens, heads, HEAD)
    value_heads = values_all.reshape(images, plan_tokens, heads, HEAD)
    scores = (
        jnp.einsum("bnhe,bmhe->bhnm", query_heads, key_heads, preferred_element_type=jnp.float32)
        * scale
    )
    maxima = jnp.max(scores, axis=-1, keepdims=True)
    expo = jnp.exp(scores - maxima)
    probs = expo / jnp.sum(expo, axis=-1, keepdims=True)
    probs_b = probs.astype(jnp.bfloat16)
    attended = jnp.einsum(
        "bhnm,bmhe->bnhe", probs_b, value_heads, preferred_element_type=jnp.float32
    )
    attended = attended.reshape(tokens_here, channels).astype(jnp.bfloat16)
    result = mixed.astype(jnp.float32) + jnp.dot(
        attended, weight_o, preferred_element_type=jnp.float32
    )
    block_out = result.astype(jnp.bfloat16).reshape(images, band_rows, columns, channels)
    grad_flat = cotangent.reshape(tokens_here, channels)
    grad_att = lax.dot_general(
        grad_flat, weight_o, (((1,), (1,)), ((), ())), preferred_element_type=jnp.float32
    )
    grad_att = grad_att.astype(jnp.bfloat16).reshape(images, band_rows * columns, heads, HEAD)
    dprob = jnp.einsum("bnhe,bmhe->bhnm", grad_att, value_heads, preferred_element_type=jnp.float32)
    dscore = (probs * (dprob - jnp.sum(probs * dprob, axis=-1, keepdims=True)) * scale).astype(
        jnp.bfloat16
    )
    dquery = jnp.einsum("bhnm,bmhe->bnhe", dscore, key_heads, preferred_element_type=jnp.float32)
    dquery = dquery.reshape(tokens_here, channels).astype(jnp.bfloat16)
    total_tokens = images * lax.axis_size("dp") * band_rows * lax.axis_size("spatial") * columns
    factor = 1.0 / math.sqrt(total_tokens)
    contract = (((0,), (0,)), ((), ()))
    grad_query = lax.dot_general(mixed, dquery, contract, preferred_element_type=jnp.float32)
    grad_output = lax.dot_general(attended, grad_flat, contract, preferred_element_type=jnp.float32)
    own_rows = lax.psum_scatter(
        jnp.stack([grad_query, grad_output], 1) * factor, "dp", scatter_dimension=0, tiled=True
    )
    weight_grads = lax.psum(own_rows, "spatial")
    return (block_out, weight_grads)


def solution(mesh):
    return jax.shard_map(
        body,
        mesh=mesh,
        in_specs=(
            P("dp", "spatial", None, None),
            P("dp", "spatial", None),
            P(None, "dp", None),
            P(),
            P(None, "dp", None),
            P("dp", "spatial", None, None),
        ),
        out_specs=(P("dp", "spatial", None, None), P("dp", None, None)),
        check_vma=False,
    )
```

profile of v0, /device:TPU:1, one launch (start us, length us, event | category | flops | bytes accessed | tf_op | source)
XLA Modules:
  0.0 876.4 jit_solution(7868620939936180710)
XLA Ops:
  8.0 1.8 copy.29
  9.8 1.0 convert_reduce_fusion
  11.2 33.4 %all-reduce.2 = (f32[2,32]{1,0:T(2,128)S(1)}, f32[2,32]{1,0:T(2,128)S(1)}) all-reduce(f32[2,32]{1,0:T(2,128)S(1)} %reduce_sum.55, f32[2,32]{1,0:T(2,128)S(1)} %reduce_sum.52), channel_id=1, replica_groups=mesh['dp'=32,'spatial'=16] {'spatial'}, use_global_device_ids=true, to_apply=%region_5.6 | all-reduce | flops 128 | bytes 1024 | tf_op jit(solution)/shard_map/psum | solution.py:38
  45.2 1.9 collective-permute-start
  47.1 2.4 collective-permute-start.1
  49.5 19.2 %all_gather.10 = bf16[2,256,640]{2,1,0:T(8,128)(2,1)S(1)} all-gather(bf16[2,16,640]{2,1,0:T(8,128)(2,1)S(1)} %copy-done.7), channel_id=1, replica_groups=mesh['dp'=32,'spatial'=16] {'spatial'}, dimensions={1}, use_global_device_ids=true | all-gather | bytes 696320 | tf_op jit(solution)/shard_map/all_gather | solution.py:73
  69.0 0.7 constant_dynamic-update-slice_fusion.8
  75.1 89.4 %all-gather.5.cloned.1.call-done = bf16[4,640,640]{2,0,1:T(4,128)(2,1)} async-done(((bf16[4,20,640]{2,0,1:T(4,128)(2,1)}), bf16[4,640,640]{2,0,1:T(4,128)(2,1)}) %all-gather.5.cloned.1.call-update) | async-done | bytes 3276816 | tf_op jit(solution)/shard_map/all_gather | solution.py:67
  164.4 12.3 %fusion.57 = (bf16[1,640,640]{2,0,1:T(2,128)(2,1)S(1)}, bf16[1,640,640]{2,0,1:T(2,128)(2,1)S(1)}, bf16[1,640,640]{2,0,1:T(2,128)(2,1)}, bf16[1,640,640]{2,0,1:T(2,128)(2,1)}) fusion(bf16[4,640,640]{2,0,1:T(4,128)(2,1)} %all-gather.5.cloned.1.call-done), kind=kLoop, calls=%fused_computation.73 | loop fusion | bytes 6553600 | tf_op jit(solution)/shard_map/slice | solution.py:71
  176.7 1.6 convolution_convert_fusion
  178.3 1.3 copy.36
  179.7 1.0 reshape_reshape.7
  180.7 2.2 convolution_convert_fusion.1
  184.0 1.4 fusion.33
  185.4 213.4 %all-gather.3.cloned.1.call-done = bf16[9,640,640]{2,0,1:T(8,128)(2,1)} async-done(((bf16[9,20,640]{2,0,1:T(8,128)(2,1)}), bf16[9,640,640]{2,0,1:T(8,128)(2,1)}) %all-gather.3.cloned.1.call-update) | async-done | bytes 7372816 | tf_op jit(solution)/shard_map/all_gather | solution.py:61
  398.8 7.7 fusion.27
  407.5 1.1 reshape.46
  408.7 2.6 fusion.60
  411.3 2.5 fusion.19
  413.8 9.3 %fusion.20 = bf16[2,64,10,64]{1,3,2,0:T(8,128)(2,1)S(1)} fusion(f32[2,10,64,256]{3,2,1,0:T(8,128)} %fusion.33, bf16[2,256,10,64]{1,0,3,2:T(2,128)(2,1)S(1)} %copy-done.3, f32[2,10,64,256]{3,2,1,0:T(8,128)} %get-tuple-element.27, f32[2,10,64]{2,1,0:T(8,128)S(1)} %get-tuple-element.26), kind=kOutput, calls=%fused_computation.25 | convolution fusion | flops 44320256 | bytes 3445760 | tf_op jit(solution)/shard_map/bhnm,bmhe->bnhe/dot_general | solution.py:110
  423.4 0.8 convert_element_type.78
  424.3 1.4 convolution_bitcast_fusion.1
  425.7 2.0 copy.40
  427.7 1.8 convert_element_type.72
  429.6 1.3 convolution_bitcast_fusion
  431.2 4.3 copy.47
  435.6 1.3 dynamic-slice
  437.6 285.5 %all-reduce.8.cloned.1.call-done = f32[640,2,640]{2,1,0:T(2,128)} async-done(((f32[640,2,640]{2,1,0:T(2,128)}), f32[640,2,640]{2,1,0:T(2,128)}) %all-reduce.8.cloned.1.call-update) | async-done | bytes 3276816
  723.1 1.5 constant_dynamic-slice_fusion
  724.6 1.0 fusion.26
  725.7 142.7 %all-reduce.6.cloned.1.call-done = f32[20,2,640]{2,1,0:T(2,128)} async-done(((f32[20,2,640]{2,1,0:T(2,128)}), f32[20,2,640]{2,1,0:T(2,128)}) %all-reduce.6.cloned.1.call-update) | async-done | bytes 102416 | tf_op jit(solution)/shard_map/psum | solution.py:120
  868.3 1.5 copy.107
  (57 shorter events, 10.3 us)
Async XLA Ops:
  7.2 176.2 %copy-start = (bf16[2,2,32,640]{3,2,1,0:T(8,128)(2,1)S(1)}, bf16[2,2,32,640]{3,2,1,0:T(8,128)(2,1)}, u32[]{:S(2)}) copy-start(bf16[2,2,32,640]{3,2,1,0:T(8,128)(2,1)} %param.11) | copy-start | bytes 491524
  7.2 37.8 %copy-start.4 = (bf16[2,2,32,640]{3,2,1,0:T(8,128)(2,1)S(1)}, bf16[2,2,32,640]{3,2,1,0:T(8,128)(2,1)}, u32[]{:S(2)}) copy-start(bf16[2,2,32,640]{3,2,1,0:T(8,128)(2,1)} %param.6) | copy-start | bytes 491524
  7.2 37.8 %copy-start.8 = (f32[640]{0:T(1024)S(1)}, f32[640]{0:T(1024)}, u32[]{:S(2)}) copy-start(f32[640]{0:T(1024)} %param.9) | copy-start | bytes 7684
  7.2 42.3 %copy-start.7 = (bf16[2,16,640]{2,1,0:T(8,128)(2,1)S(1)}, bf16[2,16,640]{2,1,0:T(8,128)(2,1)}, u32[]{:S(2)}) copy-start(bf16[2,16,640]{2,1,0:T(8,128)(2,1)} %param.7) | copy-start | bytes 122884
  7.2 157.2 %all-gather.5.cloned.1.call-start = ((), (), s32[]{:S(2)}) async-start(), calls=%async_computation.1 | async-start | bytes 3379200 | tf_op jit(solution)/shard_map/all_gather | solution.py:67
  7.9 390.9 %all-gather.3.cloned.1.call-start = ((), (), s32[]{:S(2)}) async-start(), calls=%async_computation | async-start | bytes 13516800 | tf_op jit(solution)/shard_map/all_gather | solution.py:61
  9.8 713.3 %all-reduce.8.cloned.1.call-start = ((), (), s32[]{:S(2)}) async-start(), calls=%async_computation.3 | async-start | bytes 6553600
  45.2 23.5 %collective-permute-start = (bf16[2,1,32,640]{3,2,1,0:T(8,128)(2,1)S(1)}, bf16[2,1,32,640]{3,2,1,0:T(8,128)(2,1)S(1)}, u32[]{:S(2)}, u32[]{:S(2)}) collective-permute-start(bf16[2,1,32,640]{3,2,1,0:T(8,128)(2,1)S(1)} %get-tuple-element.22), channel_id=1, source_target_pairs={{0,1},{1,2},{2,3},{3,4},{4,5},{5,6},{6,7},{7,8},{8,9},{9,10},{10,1... | collective-permute-start | bytes 245768 | tf_op jit(solution)/shard_map/ppermute | solution.py:20
  47.1 21.6 %collective-permute-start.1 = (bf16[2,1,32,640]{3,2,1,0:T(8,128)(2,1)S(1)}, bf16[2,1,32,640]{3,2,1,0:T(8,128)(2,1)S(1)}, u32[]{:S(2)}, u32[]{:S(2)}) collective-permute-start(bf16[2,1,32,640]{3,2,1,0:T(8,128)(2,1)S(1)} %get-tuple-element.23), channel_id=1, source_target_pairs={{1,0},{2,1},{3,2},{4,3},{5,4},{6,5},{7,6},{8,7},{9,8},{10,9},{11,1... | collective-permute-start | bytes 245768 | tf_op jit(solution)/shard_map/ppermute | solution.py:22
  398.8 8.4 copy-start.1
  406.6 0.7 copy-start.5
  406.6 2.1 copy-start.3
  435.5 289.1 %copy-start.2 = (bf16[128,640]{0,1:T(8,128)(2,1)S(1)}, bf16[128,640]{0,1:T(8,128)(2,1)}, u32[]{:S(2)}) copy-start(bf16[128,640]{0,1:T(8,128)(2,1)} %convert_element_type.72) | copy-start | bytes 491524
  435.5 289.1 %copy-start.6 = (bf16[128,640]{1,0:T(8,128)(2,1)S(1)}, bf16[128,640]{1,0:T(8,128)(2,1)}, u32[]{:S(2)}) copy-start(bf16[128,640]{1,0:T(8,128)(2,1)} %copy-done.5) | copy-start | bytes 491524
  435.5 432.8 %all-reduce.6.cloned.1.call-start = ((), (), s32[]{:S(2)}) async-start(), calls=%async_computation.2 | async-start | bytes 204800 | tf_op jit(solution)/shard_map/psum | solution.py:120
Sparse Core Ops, SparseCore 0:
  11.1 153.2 all-gather.4
  167.5 231.2 all-gather.2
  435.6 287.3 all-reduce.7
  726.4 141.8 all-reduce.5
where the time goes:
time: 877 us; the launch traced here: 876 us
  waiting for transfers between devices  732 us (83%)
  blocking collectives  52.6 us (6%)
  local copies, waits for them, and re-layouts  39.4 us (4%)
  matrix products  31.7 us (4%)
  between operations  14.7 us (2%)
    unnamed x5, waiting for transfers between devices  286 us
    all_gather x1, waiting for transfers between devices, body(): lax.all_gather(conv_weight, 'dp', axis=1, tiled=True)  213 us
    psum x1, waiting for transfers between devices, body(): weight_grads = lax.psum(own_rows, 'spatial')  143 us
    all_gather x1, waiting for transfers between devices, body(): weights = lax.all_gather(attn_weights, 'dp', axis=1, tiled=True)  89.4 us
    psum x1, blocking collectives, body(): first_sums, second_sums = lax.psum((first_sums, second_sums), 'spatial')  33.4 us
    all_gather x1, blocking collectives, body(): plan_all = lax.all_gather(plan, 'spatial', axis=1, tiled=True)  19.2 us
  transfers between devices with their start and end apart: 6, of which 4 were waited for; matrix products, arithmetic and copies ran while one was open for 4% of the time, Pallas kernels for 0%

commit v1 on v0

--- a/solution.py
+++ b/solution.py
@@ -117,7 +117,7 @@
     own_rows = lax.psum_scatter(
         jnp.stack([grad_query, grad_output], 1) * factor, "dp", scatter_dimension=0, tiled=True
     )
-    weight_grads = lax.psum(own_rows, "spatial")
+    weight_grads = jnp.sum(lax.all_gather(own_rows, "spatial"), axis=0)
     return (block_out, weight_grads)
 
 

time: 877 us -> 790 us (0.901)
  waiting for transfers between devices: 732 us -> 643 us
    psum x1 -> x0, waiting for transfers between devices: 143 us -> none  [body(): weight_grads = lax.psum(own_rows, 'spatial')]
    all_gather x0 -> x1, waiting for transfers between devices: none -> 54.4 us  [body(): weight_grads = jnp.sum(lax.all_gather(own_rows, 'spatial'), axis=0)]
where the time goes in v1:
time: 790 us; the launch traced here: 789 us
  waiting for transfers between devices  643 us (81%)
  blocking collectives  52.6 us (7%)
  local copies, waits for them, and re-layouts  37.9 us (5%)
  matrix products  31.7 us (4%)
  between operations  14.7 us (2%)
    unnamed x5, waiting for transfers between devices  286 us
    all_gather x1, waiting for transfers between devices, body(): lax.all_gather(conv_weight, 'dp', axis=1, tiled=True)  213 us
    all_gather x1, waiting for transfers between devices, body(): weights = lax.all_gather(attn_weights, 'dp', axis=1, tiled=True)  89.4 us
    all_gather x1, waiting for transfers between devices, body(): weight_grads = jnp.sum(lax.all_gather(own_rows, 'spatial'), axis=0)  54.4 us
    psum x1, blocking collectives, body(): first_sums, second_sums = lax.psum((first_sums, second_sums), 'spatial')  33.4 us
    all_gather x1, blocking collectives, body(): plan_all = lax.all_gather(plan, 'spatial', axis=1, tiled=True)  19.2 us
  transfers between devices with their start and end apart: 6, of which 4 were waited for; matrix products, arithmetic and copies ran while one was open for 4% of the time, Pallas kernels for 0%

profile of v1, /device:TPU:1, one launch (start us, length us, event | category | flops | bytes accessed | tf_op | source)
XLA Modules:
  0.0 789.2 jit_solution(6531288617233358421)
XLA Ops:
  8.0 1.8 copy.28
  9.8 1.0 convert_reduce_fusion
  11.2 33.4 %all-reduce.2 = (f32[2,32]{1,0:T(2,128)S(1)}, f32[2,32]{1,0:T(2,128)S(1)}) all-reduce(f32[2,32]{1,0:T(2,128)S(1)} %reduce_sum.64, f32[2,32]{1,0:T(2,128)S(1)} %reduce_sum.61), channel_id=1, replica_groups=mesh['dp'=32,'spatial'=16] {'spatial'}, use_global_device_ids=true, to_apply=%region_5.6 | all-reduce | flops 128 | bytes 1024 | tf_op jit(solution)/shard_map/psum | solution.py:38
  45.2 1.9 collective-permute-start
  47.1 2.4 collective-permute-start.1
  49.5 19.2 %all_gather.16 = bf16[2,256,640]{2,1,0:T(8,128)(2,1)S(1)} all-gather(bf16[2,16,640]{2,1,0:T(8,128)(2,1)S(1)} %copy-done.7), channel_id=1, replica_groups=mesh['dp'=32,'spatial'=16] {'spatial'}, dimensions={1}, use_global_device_ids=true | all-gather | bytes 696320 | tf_op jit(solution)/shard_map/all_gather | solution.py:73
  69.0 0.7 constant_dynamic-update-slice_fusion.8
  75.1 89.4 %all-gather.7.cloned.1.call-done = bf16[4,640,640]{2,0,1:T(4,128)(2,1)} async-done(((bf16[4,20,640]{2,0,1:T(4,128)(2,1)}), bf16[4,640,640]{2,0,1:T(4,128)(2,1)}) %all-gather.7.cloned.1.call-update) | async-done | bytes 3276816 | tf_op jit(solution)/shard_map/all_gather | solution.py:67
  164.4 12.3 %fusion.57 = (bf16[1,640,640]{2,0,1:T(2,128)(2,1)S(1)}, bf16[1,640,640]{2,0,1:T(2,128)(2,1)S(1)}, bf16[1,640,640]{2,0,1:T(2,128)(2,1)}, bf16[1,640,640]{2,0,1:T(2,128)(2,1)}) fusion(bf16[4,640,640]{2,0,1:T(4,128)(2,1)} %all-gather.7.cloned.1.call-done), kind=kLoop, calls=%fused_computation.73 | loop fusion | bytes 6553600 | tf_op jit(solution)/shard_map/slice | solution.py:71
  176.7 1.6 convolution_convert_fusion
  178.3 1.3 copy.35
  179.7 1.0 reshape_reshape.7
  180.7 2.2 convolution_convert_fusion.1
  184.0 1.4 fusion.33
  185.4 213.4 %all-gather.5.cloned.1.call-done = bf16[9,640,640]{2,0,1:T(8,128)(2,1)} async-done(((bf16[9,20,640]{2,0,1:T(8,128)(2,1)}), bf16[9,640,640]{2,0,1:T(8,128)(2,1)}) %all-gather.5.cloned.1.call-update) | async-done | bytes 7372816 | tf_op jit(solution)/shard_map/all_gather | solution.py:61
  398.8 7.7 fusion.27
  407.5 1.1 reshape.47
  408.7 2.6 fusion.60
  411.3 2.5 fusion.19
  413.8 9.3 %fusion.20 = bf16[2,64,10,64]{1,3,2,0:T(8,128)(2,1)S(1)} fusion(f32[2,10,64,256]{3,2,1,0:T(8,128)} %fusion.33, bf16[2,256,10,64]{1,0,3,2:T(2,128)(2,1)S(1)} %copy-done.3, f32[2,10,64,256]{3,2,1,0:T(8,128)} %get-tuple-element.23, f32[2,10,64]{2,1,0:T(8,128)S(1)} %get-tuple-element.22), kind=kOutput, calls=%fused_computation.25 | convolution fusion | flops 44320256 | bytes 3445760 | tf_op jit(solution)/shard_map/bhnm,bmhe->bnhe/dot_general | solution.py:110
  423.4 0.8 convert_element_type.78
  424.3 1.4 convolution_bitcast_fusion.1
  425.7 2.0 copy.39
  427.7 1.8 convert_element_type.72
  429.6 1.3 convolution_bitcast_fusion
  431.2 4.3 copy.46
  435.6 1.3 dynamic-slice
  437.6 285.5 %all-reduce.5.cloned.1.call-done = f32[640,2,640]{2,1,0:T(2,128)} async-done(((f32[640,2,640]{2,1,0:T(2,128)}), f32[640,2,640]{2,1,0:T(2,128)}) %all-reduce.5.cloned.1.call-update) | async-done | bytes 3276816
  723.1 1.5 constant_dynamic-slice_fusion
  724.6 1.0 fusion.26
  725.7 54.4 %all-gather.9.cloned.1.call-done = f32[320,2,640]{2,1,0:T(2,128)} async-done(((f32[20,2,640]{2,1,0:T(2,128)}), f32[320,2,640]{2,1,0:T(2,128)}) %all-gather.9.cloned.1.call-update) | async-done | bytes 1638416 | tf_op jit(solution)/shard_map/all_gather | solution.py:120
  780.1 2.6 reduce_sum.67
  (57 shorter events, 10.3 us)
Async XLA Ops:
  7.2 176.2 %copy-start = (bf16[2,2,32,640]{3,2,1,0:T(8,128)(2,1)S(1)}, bf16[2,2,32,640]{3,2,1,0:T(8,128)(2,1)}, u32[]{:S(2)}) copy-start(bf16[2,2,32,640]{3,2,1,0:T(8,128)(2,1)} %param.11) | copy-start | bytes 491524
  7.2 37.8 %copy-start.4 = (bf16[2,2,32,640]{3,2,1,0:T(8,128)(2,1)S(1)}, bf16[2,2,32,640]{3,2,1,0:T(8,128)(2,1)}, u32[]{:S(2)}) copy-start(bf16[2,2,32,640]{3,2,1,0:T(8,128)(2,1)} %param.6) | copy-start | bytes 491524
  7.2 37.8 %copy-start.8 = (f32[640]{0:T(1024)S(1)}, f32[640]{0:T(1024)}, u32[]{:S(2)}) copy-start(f32[640]{0:T(1024)} %param.9) | copy-start | bytes 7684
  7.2 42.3 %copy-start.7 = (bf16[2,16,640]{2,1,0:T(8,128)(2,1)S(1)}, bf16[2,16,640]{2,1,0:T(8,128)(2,1)}, u32[]{:S(2)}) copy-start(bf16[2,16,640]{2,1,0:T(8,128)(2,1)} %param.7) | copy-start | bytes 122884
  7.2 157.2 %all-gather.7.cloned.1.call-start = ((), (), s32[]{:S(2)}) async-start(), calls=%async_computation.1 | async-start | bytes 3379200 | tf_op jit(solution)/shard_map/all_gather | solution.py:67
  7.9 390.9 %all-gather.5.cloned.1.call-start = ((), (), s32[]{:S(2)}) async-start(), calls=%async_computation | async-start | bytes 13516800 | tf_op jit(solution)/shard_map/all_gather | solution.py:61
  9.8 713.3 %all-reduce.5.cloned.1.call-start = ((), (), s32[]{:S(2)}) async-start(), calls=%async_computation.3 | async-start | bytes 6553600
  45.2 23.5 %collective-permute-start = (bf16[2,1,32,640]{3,2,1,0:T(8,128)(2,1)S(1)}, bf16[2,1,32,640]{3,2,1,0:T(8,128)(2,1)S(1)}, u32[]{:S(2)}, u32[]{:S(2)}) collective-permute-start(bf16[2,1,32,640]{3,2,1,0:T(8,128)(2,1)S(1)} %get-tuple-element.18), channel_id=1, source_target_pairs={{0,1},{1,2},{2,3},{3,4},{4,5},{5,6},{6,7},{7,8},{8,9},{9,10},{10,1... | collective-permute-start | bytes 245768 | tf_op jit(solution)/shard_map/ppermute | solution.py:20
  47.1 21.6 %collective-permute-start.1 = (bf16[2,1,32,640]{3,2,1,0:T(8,128)(2,1)S(1)}, bf16[2,1,32,640]{3,2,1,0:T(8,128)(2,1)S(1)}, u32[]{:S(2)}, u32[]{:S(2)}) collective-permute-start(bf16[2,1,32,640]{3,2,1,0:T(8,128)(2,1)S(1)} %get-tuple-element.19), channel_id=1, source_target_pairs={{1,0},{2,1},{3,2},{4,3},{5,4},{6,5},{7,6},{8,7},{9,8},{10,9},{11,1... | collective-permute-start | bytes 245768 | tf_op jit(solution)/shard_map/ppermute | solution.py:22
  398.8 8.4 %copy-start.1 = (bf16[1,640,640]{2,0,1:T(2,128)(2,1)S(1)}, bf16[1,640,640]{2,0,1:T(2,128)(2,1)}, u32[]{:S(2)}) copy-start(bf16[1,640,640]{2,0,1:T(2,128)(2,1)} %get-tuple-element.8) | copy-start | bytes 2457604
  406.6 0.7 copy-start.5
  406.6 2.1 copy-start.3
  435.5 289.1 %copy-start.2 = (bf16[128,640]{0,1:T(8,128)(2,1)S(1)}, bf16[128,640]{0,1:T(8,128)(2,1)}, u32[]{:S(2)}) copy-start(bf16[128,640]{0,1:T(8,128)(2,1)} %convert_element_type.72) | copy-start | bytes 491524
  435.5 289.1 %copy-start.6 = (bf16[128,640]{1,0:T(8,128)(2,1)S(1)}, bf16[128,640]{1,0:T(8,128)(2,1)}, u32[]{:S(2)}) copy-start(bf16[128,640]{1,0:T(8,128)(2,1)} %copy-done.5) | copy-start | bytes 491524
  435.5 344.6 %all-gather.9.cloned.1.call-start = ((), (), s32[]{:S(2)}) async-start(), calls=%async_computation.2 | async-start | bytes 1740800 | tf_op jit(solution)/shard_map/all_gather | solution.py:120
Sparse Core Ops, SparseCore 0:
  11.1 153.2 all-gather.6
  167.5 231.2 all-gather.4
  435.6 287.3 all-reduce.4
  725.6 54.4 all-gather.8
